TPU v7x, 32 devices: a whole 2x2x4 slice. The times are simulated.
32 devices in a mesh: row: 4 (over y, core), col: 8 (over z, x).
Axes of the slice: x: 2, y: 2, z: 4, core: 2. Of those that a mesh axis runs over, the one named last changes fastest.
Arguments:
- hess_inv: float32 [16384, 16384], P('row', 'col'), as said below
- weights: bfloat16 [6144, 16384], P('row', 'col'), may hold values from -6 to 6
- removed: int32 [128], replicated, may hold values from 0 to 16383, as said below
Outputs:
- hess_out: float32 [16384, 16384], P('row', 'col')
- weight_out: bfloat16 [6144, 16384], P('row', 'col')
Inputs may be any that keep to these rules, and one draw needn't show every extreme that they name: `removed`: sorted ascending and distinct; each aligned block of 2048 columns holds at most 48 of them, and at least one block holds exactly 48. `hess_inv`: symmetric and positive definite.
All inputs are finite; a program needn't handle non-finite values.
Results may differ from a plain program's by a relative error of at most 0.005.
Values may be sent and summed in bfloat16 or wider, within the bound.
No kernel may reach another device: no remote copies, remote signals or barrier semaphores. Data moves between devices by JAX's collectives and lax.ppermute only.
A program may use at most 128 MiB of HBM per device.

v0:
```python
import jax
import jax.numpy as jnp
from jax import lax
from jax.sharding import PartitionSpec as P

MOST = 48


def spread(block, axis, owner):
    block = jnp.where(lax.axis_index(axis) == owner, block, jnp.zeros_like(block))
    return lax.psum(block, axis)


def pick_owned(source, removed, tile_index, tile_size, slot_count, which_axis):
    before = jnp.sum((removed < tile_index * tile_size).astype(jnp.int32))
    within = jnp.sum((removed // tile_size == tile_index).astype(jnp.int32))
    slot_rank = jnp.arange(slot_count, dtype=jnp.int32)
    chosen = jnp.clip(before + slot_rank, 0, removed.shape[0] - 1)
    local_col = jnp.clip(removed[chosen] - tile_index * tile_size, 0, tile_size - 1)
    taken_part = jnp.take(source, local_col, axis=which_axis)
    live_slot = slot_rank < within
    mask_shape = [1, 1]
    mask_shape[which_axis] = slot_count
    return jnp.where(live_slot.reshape(mask_shape), taken_part, jnp.zeros((), taken_part.dtype))


def slot_map(removed, tile_size, slot_count):
    which_tile = removed // tile_size
    first_pos = jnp.sum(
        (removed[None, :] < (which_tile * tile_size)[:, None]).astype(jnp.int32), axis=1
    )
    position = jnp.arange(removed.shape[0], dtype=jnp.int32)
    return which_tile * slot_count + position - first_pos


def on_device(hess_inv, weights, removed):
    row_count = lax.axis_size("row")
    col_count = lax.axis_size("col")
    row_index = lax.axis_index("row")
    col_index = lax.axis_index("col")
    row_tile, col_tile = hess_inv.shape
    tile_ratio = col_count // row_count
    col_slots = slot_map(removed, col_tile, MOST)
    packed_weight = pick_owned(weights, removed, col_index, col_tile, MOST, 1)
    packed_rows = pick_owned(hess_inv, removed, row_index, row_tile, tile_ratio * MOST, 0)
    gathered = lax.all_gather(packed_rows, "row", axis=0, tiled=True)
    upper_rows = jnp.take(gathered, slot_map(removed, row_tile, tile_ratio * MOST), axis=0)
    pieces = [
        spread(upper_rows.astype(jnp.bfloat16), "col", row_index * tile_ratio + offset).astype(
            upper_rows.dtype
        )
        for offset in range(tile_ratio)
    ]
    left_rows = jnp.concatenate(pieces, axis=1)
    weight_wide = lax.all_gather(packed_weight, "col", axis=1, tiled=True)
    weight_left = jnp.take(weight_wide, col_slots, axis=1)
    own_cols = pick_owned(upper_rows, removed, col_index, col_tile, MOST, 1)
    block_wide = lax.all_gather(own_cols, "col", axis=1, tiled=True)
    removed_block = jnp.take(block_wide, col_slots, axis=1)
    factor = jnp.linalg.cholesky(removed_block)
    identity = jnp.eye(removed_block.shape[0], dtype=jnp.float32)
    factor_inv = jax.scipy.linalg.solve_triangular(factor, identity, lower=True)
    block_inv = jnp.dot(factor_inv.T, factor_inv, precision=lax.Precision.HIGHEST)
    coupling = jnp.dot(block_inv, upper_rows, precision=lax.Precision.HIGHEST)
    correction = lax.dot_general(
        left_rows, coupling, (((0,), (0,)), ((), ())), precision=lax.Precision.HIGHEST
    )
    hess_out = hess_inv - correction
    weight_fix = jnp.dot(weight_left.astype(jnp.float32), coupling, precision=lax.Precision.HIGHEST)
    weight_out = (weights.astype(jnp.float32) - weight_fix).astype(jnp.bfloat16)
    return (hess_out, weight_out)


def solution(mesh):
    placed = (P("row", "col"), P("row", "col"), P())
    return jax.shard_map(
        on_device,
        mesh=mesh,
        in_specs=placed,
        out_specs=(P("row", "col"), P("row", "col")),
        check_vma=False,
    )
```

profile of v0, /device:TPU:0, one launch (start us, length us, event | category | flops | bytes accessed | tf_op | source)
XLA Modules:
  0.0 271.6 jit_solution(3088426548601150920)
XLA Ops:
  7.2 0.0 all-gather.5.cloned.1.call-start
  7.2 1.4 fusion.12
  8.6 0.7 fusion.16
  9.3 1.4 gather_fusion.3
  10.8 0.7 iota_compare_fusion.3
  11.4 0.0 copy-start
  11.4 8.6 %copy.13 = bf16[1536,2048]{0,1:T(8,128)(2,1)} copy(bf16[1536,2048]{1,0:T(8,128)(2,1)} %param.4) | data formatting | bytes 12582912 | tf_op args[1]
  20.0 4.4 %gather_fusion.6 = bf16[48,1536]{1,0:T(8,128)(2,1)S(1)} fusion(bf16[1536,2048]{0,1:T(8,128)(2,1)} %copy.13, s32[1024]{0:T(1024)S(1)} %pad_clamp_fusion.1), kind=kCustom, calls=%fused_computation.6 | custom fusion | bytes 295104 | tf_op jit(solution)/shard_map/jit(_take)/gather | solution.py:20
  24.4 0.8 select_bitcast_fusion
  25.2 0.0 all-gather.5.cloned.1.call-update
  25.2 0.0 all-gather.3.cloned.1.call-start
  25.3 0.7 fusion.14
  26.0 0.0 copy-done
  26.0 1.2 gather_fusion
  27.3 11.9 %gather_fusion.1 = f32[96,2048]{1,0:T(8,128)S(1)} fusion(f32[4096,2048]{1,0:T(8,128)} %param.3, s32[1024]{0:T(1024)S(1)} %pad_clamp_fusion.4), kind=kCustom, calls=%fused_computation.1 | custom fusion | bytes 1573248 | tf_op jit(solution)/shard_map/jit(_take)/gather | solution.py:20
  39.2 0.6 fusion.10
  39.8 0.6 iota_compare_fusion.4
  40.5 1.0 select_select_fusion
  41.5 0.0 all-gather.3.cloned.1.call-update
  41.6 0.0 all-reduce.3.cloned.1.call-start
  41.6 0.2 convert_reduce_fusion
  41.9 27.4 %all-gather.5.cloned.1.call-done = bf16[1536,384]{0,1:T(8,128)(2,1)} async-done(((bf16[1536,48]{0,1:T(8,128)(2,1)}), bf16[1536,384]{0,1:T(8,128)(2,1)}) %all-gather.5.cloned.1.call-update) | async-done | bytes 1179664 | tf_op jit(solution)/shard_map/all_gather | solution.py:55
  69.2 2.7 gather_fusion.7
  71.9 26.7 %all-gather.3.cloned.1.call-done = f32[384,2048]{1,0:T(8,128)} async-done(((f32[96,2048]{1,0:T(8,128)}), f32[384,2048]{1,0:T(8,128)}) %all-gather.3.cloned.1.call-update) | async-done | bytes 3145744 | tf_op jit(solution)/shard_map/all_gather | solution.py:46
  98.6 3.3 %gather_fusion.2 = f32[128,2048]{1,0:T(8,128)S(1)} fusion(f32[384,2048]{1,0:T(8,128)} %all-gather.3.cloned.1.call-done, s32[1024]{0:T(1024)S(1)} %pad_clamp_fusion.3), kind=kCustom, calls=%fused_computation.2 | custom fusion | bytes 2097664 | tf_op jit(solution)/shard_map/jit(_take)/gather | solution.py:47
  101.9 1.0 broadcast_select_fusion.2
  102.9 0.3 copy.11
  103.2 0.9 broadcast_select_fusion.1
  104.1 0.6 gather_fusion.4
  104.7 0.1 select_bitcast_fusion.1
  104.8 30.9 %all_gather.10 = f32[128,384]{0,1:T(8,128)S(1)} all-gather(f32[128,48]{0,1:T(8,128)S(1)} %select_bitcast_fusion.1), channel_id=1, replica_groups=mesh['row'=4,'col'=8] {'col'}, dimensions={1}, use_global_device_ids=true | all-gather | bytes 221184 | tf_op jit(solution)/shard_map/all_gather | solution.py:58
  135.7 0.6 gather_fusion.5
  136.3 0.1 broadcast_select_fusion.3
  136.4 0.1 copy.12
  136.5 0.1 fusion.9
  136.6 11.7 %cholesky.16 = f32[128,128]{1,0:T(8,128)S(1)} custom-call(f32[128,128]{1,0:T(8,128)S(1)} %fusion.9), custom_call_target="Cholesky" | custom-call | tf_op jit(solution)/shard_map/jit(cholesky)/cholesky | solution.py:60
  148.3 0.6 compare_reduce_fusion
  149.0 0.7 fusion.6
  149.6 9.8 %custom-call.7 = f32[1,128,128]{1,2,0:T(8,128)S(1)} custom-call(f32[1,128,128]{2,1,0:T(8,128)S(1)} %fusion.6), custom_call_target="InvertDiagBlocksLowerTriangular" | custom-call | tf_op jit(solution)/shard_map/jit(_solve_triangular)/triangular_solve | solution.py:62
  159.5 0.3 fusion.7
  159.7 0.0 all-reduce.3.cloned.1.call-update
  159.7 0.3 fusion.20
  160.0 1.0 fusion.21
  161.0 9.6 %subtract_convert_fusion = bf16[1536,2048]{1,0:T(8,128)(2,1)} fusion(bf16[1536,2048]{1,0:T(8,128)(2,1)} %param.4, f32[128,2048]{1,0:T(8,128)S(1)} %fusion.21, bf16[128,1536]{1,0:T(8,128)(2,1)S(1)} %gather_fusion.7, pred[128]{0:T(512)(128)(4,1)S(1)} %get-tuple-element.10), kind=kOutput, calls=%fused_computation.9 | convolution fusion | flops 4841472000 | bytes 14024832 | tf_op jit(solution)/shard_map/dot_general | solution.py:69
  170.6 67.6 %all-reduce.3.cloned.1.call-done = (bf16[128,2048]{1,0:T(8,128)(2,1)}, bf16[128,2048]{1,0:T(8,128)(2,1)}) async-done(((bf16[128,2048]{1,0:T(8,128)(2,1)}, bf16[128,2048]{1,0:T(8,128)(2,1)}), (bf16[128,2048]{1,0:T(8,128)(2,1)}, bf16[128,2048]{1,0:T(8,128)(2,1)})) %all-reduce.3.cloned.1.call-update) | async-done | bytes 1048592 | tf_op jit(solution)/shard_map/psum | solution.py:11
  238.2 26.9 %convolution_subtract_fusion = f32[4096,2048]{1,0:T(8,128)} fusion(f32[4096,2048]{1,0:T(8,128)} %param.3, f32[128,2048]{1,0:T(8,128)S(1)} %fusion.21, bf16[128,2048]{1,0:T(8,128)(2,1)} %get-tuple-element.6, bf16[128,2048]{1,0:T(8,128)(2,1)} %get-tuple-element.7), kind=kOutput, calls=%fused_computation.8 | convolution fusion | flops 12895387648 | bytes 69206016 | tf_op jit(solution)/shard_map/dot_general | solution.py:65
  (13 shorter events, 0.1 us)
Async XLA Ops:
  7.2 62.1 %all-gather.5.cloned.1.call-start = ((), (), s32[]{:S(2)}) async-start(), calls=%async_computation.1 | async-start | bytes 1327104 | tf_op jit(solution)/shard_map/all_gather | solution.py:55
  11.4 14.6 %copy-start = (s32[128]{0:T(128)S(1)}, s32[128]{0:T(128)}, u32[]{:S(2)}) copy-start(s32[128]{0:T(128)} %param.5) | copy-start | bytes 1540
  25.2 73.4 %all-gather.3.cloned.1.call-start = ((), (), s32[]{:S(2)}) async-start(), calls=%async_computation | async-start | bytes 3932160 | tf_op jit(solution)/shard_map/all_gather | solution.py:46
  41.6 196.6 %all-reduce.3.cloned.1.call-start = ((), (), s32[]{:S(2)}) async-start(), calls=%async_computation.2 | async-start | bytes 2097152 | tf_op jit(solution)/shard_map/psum | solution.py:11
Sparse Core Ops, SparseCore 0:
  25.3 43.8 all-gather.4
  71.4 27.1 all-gather.2
  159.9 78.2 all-reduce.2
where the time goes:
time: 272 us
  waiting for transfers between devices  122 us (45%)
  matrix products  38 us (14%)
  local copies, waits for them, and re-layouts  35.3 us (13%)
  other arithmetic  31.7 us (12%)
  blocking collectives  30.9 us (11%)
  between operations  14 us (5%)
    psum x1, waiting for transfers between devices, spread(): return lax.psum(block, axis)  67.6 us
    all_gather x1, blocking collectives, on_device(): block_wide = lax.all_gather(own_cols, 'col', axis=1, tiled=True)  30.9 us
    all_gather x1, waiting for transfers between devices, on_device(): weight_wide = lax.all_gather(packed_weight, 'col', axis=1, tiled=True)  27.4 us
    dot_general x1, matrix products, on_device(): lax.dot_general(left_rows, coupling, (((0,), (0,)), ((), ())), precision=...  26.9 us
    all_gather x1, waiting for transfers between devices, on_device(): gathered = lax.all_gather(packed_rows, 'row', axis=0, tiled=True)  26.7 us
    gather x3, local copies, waits for them, and re-layouts, pick_owned(): taken_part = jnp.take(source, local_col, axis=which_axis)  16.9 us
    another operation x3, other arithmetic, on_device(): factor = jnp.linalg.cholesky(removed_block)  12.4 us
    another operation x2, other arithmetic, on_device(): factor_inv = jax.scipy.linalg.solve_triangular(factor, identity, lower=True)  10.5 us
  transfers between devices with their start and end apart: 3, of which 3 were waited for; matrix products, arithmetic and copies ran while one was open for 11% of the time, Pallas kernels for 0%

commit v1 on v0

--- a/solution.py
+++ b/solution.py
@@ -8,7 +8,7 @@
 
 def spread(block, axis, owner):
     block = jnp.where(lax.axis_index(axis) == owner, block, jnp.zeros_like(block))
-    return lax.psum(block, axis)
+    return jnp.sum(lax.all_gather(block, axis), axis=0)
 
 
 def pick_owned(source, removed, tile_index, tile_size, slot_count, which_axis):

time: 272 us -> 286 us (1.051)
  waiting for transfers between devices: 122 us -> 129 us
  other arithmetic: 31.7 us -> 36.9 us
    all_gather x0 -> x2, waiting for transfers between devices: none -> 75.2 us  [spread(): return jnp.sum(lax.all_gather(block, axis), axis=0)]
    psum x1 -> x0, waiting for transfers between devices: 67.6 us -> none  [spread(): return lax.psum(block, axis)]
    all_gather x1, waiting for transfers between devices: 26.7 us -> 14.7 us  [on_device(): gathered = lax.all_gather(packed_rows, 'row', axis=0, tiled=True)]
    all_gather x1, waiting for transfers between devices: 27.4 us -> 38.7 us  [on_device(): weight_wide = lax.all_gather(packed_weight, 'col', axis=1, tiled=True)]
    reduce_sum x0 -> x2, other arithmetic: none -> 5.91 us  [spread(): return jnp.sum(lax.all_gather(block, axis), axis=0)]
  transfers between devices with their start and end apart: 3 -> 4, of which waited for: 3 -> 4; matrix products, arithmetic and copies ran while one was open for 11% -> 22% of each run, Pallas kernels for 0% -> 0%
where the time goes in v1:
time: 286 us; the launch traced here: 285 us
  waiting for transfers between devices  129 us (45%)
  matrix products  37.9 us (13%)
  other arithmetic  36.9 us (13%)
  local copies, waits for them, and re-layouts  35.4 us (12%)
  blocking collectives  31.8 us (11%)
  between operations  14 us (5%)
    all_gather x2, waiting for transfers between devices, spread(): return jnp.sum(lax.all_gather(block, axis), axis=0)  75.2 us
    all_gather x1, waiting for transfers between devices, on_device(): weight_wide = lax.all_gather(packed_weight, 'col', axis=1, tiled=True)  38.7 us
    all_gather x1, blocking collectives, on_device(): block_wide = lax.all_gather(own_cols, 'col', axis=1, tiled=True)  31.8 us
    dot_general x1, matrix products, on_device(): lax.dot_general(left_rows, coupling, (((0,), (0,)), ((), ())), precision=...  26.6 us
    gather x3, local copies, waits for them, and re-layouts, pick_owned(): taken_part = jnp.take(source, local_col, axis=which_axis)  17.3 us
    all_gather x1, waiting for transfers between devices, on_device(): gathered = lax.all_gather(packed_rows, 'row', axis=0, tiled=True)  14.7 us
    another operation x3, other arithmetic, on_device(): factor = jnp.linalg.cholesky(removed_block)  12.4 us
    another operation x2, other arithmetic, on_device(): factor_inv = jax.scipy.linalg.solve_triangular(factor, identity, lower=True)  10.5 us
  transfers between devices with their start and end apart: 4, of which 4 were waited for; matrix products, arithmetic and copies ran while one was open for 22% of the time, Pallas kernels for 0%

profile of v1, /device:TPU:0, one launch (start us, length us, event | category | flops | bytes accessed | tf_op | source)
XLA Modules:
  0.0 285.3 jit_solution(7393494177504503181)
XLA Ops:
  7.2 0.0 copy-start
  7.2 0.0 all-gather.5.cloned.1.call-start
  7.2 1.4 fusion.13
  8.6 0.7 fusion.15
  9.3 1.6 gather_fusion
  10.9 0.6 fusion.11
  11.5 0.6 iota_compare_fusion.4
  12.2 11.8 %gather_fusion.1 = f32[96,2048]{1,0:T(8,128)S(1)} fusion(f32[4096,2048]{1,0:T(8,128)} %param.3, s32[1024]{0:T(1024)S(1)} %pad_clamp_fusion.4), kind=kCustom, calls=%fused_computation.1 | custom fusion | bytes 1573248 | tf_op jit(solution)/shard_map/jit(_take)/gather | solution.py:20
  23.9 1.0 select_select_fusion
  25.0 0.0 all-gather.5.cloned.1.call-update
  25.0 0.0 all-gather.11.cloned.1.call-start
  25.1 0.6 fusion.17
  25.7 0.0 copy-done
  25.7 0.8 gather_fusion.3
  26.5 8.7 %copy.16 = bf16[1536,2048]{0,1:T(8,128)(2,1)} copy(bf16[1536,2048]{1,0:T(8,128)(2,1)} %param.4) | data formatting | bytes 12582912 | tf_op args[1]
  35.2 4.9 %gather_fusion.6 = bf16[48,1536]{1,0:T(8,128)(2,1)S(1)} fusion(bf16[1536,2048]{0,1:T(8,128)(2,1)} %copy.16, s32[1024]{0:T(1024)S(1)} %pad_clamp_fusion.1), kind=kCustom, calls=%fused_computation.6 | custom fusion | bytes 295104 | tf_op jit(solution)/shard_map/jit(_take)/gather | solution.py:20
  40.1 0.5 iota_compare_fusion.3
  40.7 0.8 select_bitcast_fusion
  41.4 0.0 all-gather.11.cloned.1.call-update
  41.5 0.0 all-gather.7.cloned.1.call-start
  41.5 0.2 convert_reduce_fusion
  41.7 14.7 %all-gather.5.cloned.1.call-done = f32[384,2048]{1,0:T(8,128)} async-done(((f32[96,2048]{1,0:T(8,128)}), f32[384,2048]{1,0:T(8,128)}) %all-gather.5.cloned.1.call-update) | async-done | bytes 3145744 | tf_op jit(solution)/shard_map/all_gather | solution.py:46
  56.4 3.3 %gather_fusion.2 = f32[128,2048]{1,0:T(8,128)S(1)} fusion(f32[384,2048]{1,0:T(8,128)} %all-gather.5.cloned.1.call-done, s32[1024]{0:T(1024)S(1)} %pad_clamp_fusion.3), kind=kCustom, calls=%fused_computation.2 | custom fusion | bytes 2097664 | tf_op jit(solution)/shard_map/jit(_take)/gather | solution.py:47
  59.8 1.2 broadcast_select_fusion.2
  60.9 0.0 all-gather.7.cloned.1.call-update
  61.0 0.0 all-gather.9.cloned.1.call-start
  61.0 0.5 all-gather.9.cloned.1.call-update
  61.6 38.7 %all-gather.11.cloned.1.call-done = bf16[1536,384]{0,1:T(8,128)(2,1)} async-done(((bf16[1536,48]{0,1:T(8,128)(2,1)}), bf16[1536,384]{0,1:T(8,128)(2,1)}) %all-gather.11.cloned.1.call-update) | async-done | bytes 1179664 | tf_op jit(solution)/shard_map/all_gather | solution.py:55
  100.3 2.7 gather_fusion.7
  103.0 0.1 broadcast_select_fusion
  103.1 0.3 copy.14
  103.5 0.6 gather_fusion.4
  104.1 0.1 select_bitcast_fusion.1
  104.1 31.8 %all_gather.20 = f32[128,384]{0,1:T(8,128)S(1)} all-gather(f32[128,48]{0,1:T(8,128)S(1)} %select_bitcast_fusion.1), channel_id=1, replica_groups=mesh['row'=4,'col'=8] {'col'}, dimensions={1}, use_global_device_ids=true | all-gather | bytes 221184 | tf_op jit(solution)/shard_map/all_gather | solution.py:58
  135.9 0.6 gather_fusion.5
  136.6 0.1 broadcast_select_fusion.3
  136.7 0.1 copy.15
  136.8 0.1 fusion.10
  136.9 11.7 %cholesky.16 = f32[128,128]{1,0:T(8,128)S(1)} custom-call(f32[128,128]{1,0:T(8,128)S(1)} %fusion.10), custom_call_target="Cholesky" | custom-call | tf_op jit(solution)/shard_map/jit(cholesky)/cholesky | solution.py:60
  148.6 0.6 compare_reduce_fusion
  149.3 0.7 fusion.7
  149.9 9.8 %custom-call.7 = f32[1,128,128]{1,2,0:T(8,128)S(1)} custom-call(f32[1,128,128]{2,1,0:T(8,128)S(1)} %fusion.7), custom_call_target="InvertDiagBlocksLowerTriangular" | custom-call | tf_op jit(solution)/shard_map/jit(_solve_triangular)/triangular_solve | solution.py:62
  159.7 0.2 fusion.8
  160.0 0.3 fusion.21
  160.3 1.0 fusion.22
  161.3 9.7 %subtract_convert_fusion = bf16[1536,2048]{1,0:T(8,128)(2,1)} fusion(bf16[1536,2048]{1,0:T(8,128)(2,1)} %param.4, f32[128,2048]{1,0:T(8,128)S(1)} %fusion.22, bf16[128,1536]{1,0:T(8,128)(2,1)S(1)} %gather_fusion.7, pred[128]{0:T(512)(128)(4,1)S(1)} %get-tuple-element.6), kind=kOutput, calls=%fused_computation.9 | convolution fusion | flops 4841472000 | bytes 14024832 | tf_op jit(solution)/shard_map/dot_general | solution.py:69
  171.0 5.0 %all-gather.7.cloned.1.call-done = bf16[8,128,2048]{2,1,0:T(8,128)(2,1)} async-done(((bf16[1,128,2048]{2,1,0:T(8,128)(2,1)}), bf16[8,128,2048]{2,1,0:T(8,128)(2,1)}) %all-gather.7.cloned.1.call-update) | async-done | bytes 4194320 | tf_op jit(solution)/shard_map/all_gather | solution.py:11
  176.0 3.0 %reduce_sum.89 = bf16[128,2048]{1,0:T(8,128)(2,1)S(1)} reduce(bf16[8,128,2048]{2,1,0:T(8,128)(2,1)} %all-gather.7.cloned.1.call-done, bf16[]{:T(256)} %constant.178.clone.1), dimensions={0}, to_apply=%region_3.4 | reduce | flops 1835008 | bytes 4718594 | tf_op jit(solution)/shard_map/reduce_sum | solution.py:11
  179.0 70.2 %all-gather.9.cloned.1.call-done = bf16[8,128,2048]{2,1,0:T(8,128)(2,1)} async-done(((bf16[1,128,2048]{2,1,0:T(8,128)(2,1)}), bf16[8,128,2048]{2,1,0:T(8,128)(2,1)}) %all-gather.9.cloned.1.call-update) | async-done | bytes 4194320 | tf_op jit(solution)/shard_map/all_gather | solution.py:11
  249.2 3.0 %reduce_sum.90 = bf16[128,2048]{1,0:T(8,128)(2,1)S(1)} reduce(bf16[8,128,2048]{2,1,0:T(8,128)(2,1)} %all-gather.9.cloned.1.call-done, bf16[]{:T(256)} %constant.178.clone.1), dimensions={0}, to_apply=%region_4.5 | reduce | flops 1835008 | bytes 4718594 | tf_op jit(solution)/shard_map/reduce_sum | solution.py:11
  252.1 26.6 %convolution_subtract_fusion = f32[4096,2048]{1,0:T(8,128)} fusion(f32[4096,2048]{1,0:T(8,128)} %param.3, f32[128,2048]{1,0:T(8,128)S(1)} %fusion.22, bf16[128,2048]{1,0:T(8,128)(2,1)S(1)} %reduce_sum.90, bf16[128,2048]{1,0:T(8,128)(2,1)S(1)} %reduce_sum.89), kind=kOutput, calls=%fused_computation.8 | convolution fusion | flops 12895387648 | bytes 69206016 | tf_op jit(solution)/shard_map/dot_general | solution.py:65
  (13 shorter events, 0.1 us)
Async XLA Ops:
  7.2 18.6 %copy-start = (s32[128]{0:T(128)S(1)}, s32[128]{0:T(128)}, u32[]{:S(2)}) copy-start(s32[128]{0:T(128)} %param.5) | copy-start | bytes 1540
  7.2 49.2 %all-gather.5.cloned.1.call-start = ((), (), s32[]{:S(2)}) async-start(), calls=%async_computation | async-start | bytes 3932160 | tf_op jit(solution)/shard_map/all_gather | solution.py:46
  25.0 75.3 %all-gather.11.cloned.1.call-start = ((), (), s32[]{:S(2)}) async-start(), calls=%async_computation.3 | async-start | bytes 1327104 | tf_op jit(solution)/shard_map/all_gather | solution.py:55
  41.5 134.5 %all-gather.7.cloned.1.call-start = ((), (), s32[]{:S(2)}) async-start(), calls=%async_computation.1 | async-start | bytes 4718592 | tf_op jit(solution)/shard_map/all_gather | solution.py:11
  61.0 188.2 %all-gather.9.cloned.1.call-start = ((), (), s32[]{:S(2)}) async-start(), calls=%async_computation.2 | async-start | bytes 4718592 | tf_op jit(solution)/shard_map/all_gather | solution.py:11
Sparse Core Ops, SparseCore 0:
  25.1 31.2 all-gather.4
  59.2 41.1 all-gather.10
  103.0 72.9 all-gather.6
  178.0 71.1 all-gather.8
